TPU v7x, 256 devices: a whole 4x4x8 slice. The times are simulated.
256 devices in a mesh: seg: 8 (over x, z_lo), bond: 32 (over z_hi, y, core).
Axes of the slice: x: 4, y: 4, z: 8 (z_hi: 4, z_lo: 2; z = z_hi * 2 + z_lo), core: 2. Of those that a mesh axis runs over, the one named last changes fastest.
Arguments:
- last_sites: bfloat16 [8, 1024, 2048], P('seg', 'bond'), may hold values from -6 to 6
- first_sites: bfloat16 [8, 1024, 2048], P('seg', 'bond'), may hold values from -0.1875 to 0.1875
- start_basis: float32 [2048, 256], replicated, may hold values from -6 to 6
- fields: float32 [8, 2], replicated, may hold values from -3 to 3
- ranks: int32 [8], replicated, may hold values from 128 to 256
Outputs:
- new_left: float32 [8, 2048, 256], P('seg', 'bond')
- new_right: float32 [8, 256, 2048], P('seg')
All inputs are finite; a program needn't handle non-finite values.
Results may differ from a plain program's by a relative error of at most 0.00035.
Values may be sent and summed in bfloat16 or wider, within the bound.
A program may use at most 64 MiB of HBM per device.

v0:
```python
import jax
import jax.numpy as jnp
from jax import lax
from jax.sharding import Mesh
from jax.sharding import PartitionSpec as P

ITERS = 4
BOND = ("bond_0", "bond_1", "bond_2")
time_step = 0.5
anisotropy = 0.6


def padded_to(lines, peers):
    spare = -len(lines) % peers
    return jnp.pad(lines, [(0, spare)] + [(0, 0)] * (lines.ndim - 1))


def sent_to_all(x, axis):
    peers = lax.axis_size(axis)
    return lax.all_to_all(jnp.broadcast_to(x[None], (peers, *x.shape)), axis, 0, 0, tiled=True)


def laid_out(pieces, dim):
    pieces = jnp.moveaxis(pieces, 0, dim)
    lengths = pieces.shape
    return pieces.reshape(*lengths[:dim], lengths[dim] * lengths[dim + 1], *lengths[dim + 2 :])


def gathered_by_axis(x, axes, dim):
    far, near = axes
    initial = sent_to_all(x, far)
    pieces = jnp.swapaxes(sent_to_all(initial, near), 0, 1)
    return laid_out(pieces.reshape(-1, *x.shape), dim)


def split_up(x, dim, peers):
    before, after = (x.shape[:dim], x.shape[dim + 1 :])
    return jnp.moveaxis(x.reshape(*before, peers, -1, *after), dim, 0)


def sent_and_summed(x, axis, dim):
    peers = lax.axis_size(axis)
    pieces = lax.all_to_all(split_up(x, dim, peers), axis, 0, 0, tiled=True)
    return jnp.sum(pieces, axis=0)


def sum_by_axis(x, axes, dim):
    far, near = axes
    pieces = split_up(x, dim, lax.axis_size(far))
    nearer = sent_and_summed(pieces, near, dim + 1)
    arrived = lax.all_to_all(nearer, far, split_axis=0, concat_axis=0, tiled=True)
    return arrived.sum(axis=0)


def sum_by_parts(x, axes):
    lines = x.reshape(-1, x.shape[-1])
    padded = padded_to(lines, lax.axis_size(axes[0]) * lax.axis_size(axes[1]))
    whole = gathered_by_axis(sum_by_axis(padded, axes, 0), axes, 0)
    return lax.slice_in_dim(whole, 0, len(lines)).reshape(x.shape)


def passed_along(x, axis, by):
    peers = lax.axis_size(axis)
    return lax.ppermute(x, axis, [(i, (i + by) % peers) for i in range(peers)])


def bond_gate(pair):
    left_field = pair[0]
    right_field = pair[1]
    half_diff = 0.5 * (left_field - right_field)
    width = jnp.sqrt(half_diff * half_diff + 0.25)
    factor = jnp.exp(time_step * anisotropy / 4.0)
    cosine = jnp.cosh(time_step * width)
    ratio = jnp.sinh(time_step * width) / width
    total = left_field + right_field
    zero = jnp.zeros((), jnp.float32)
    first = jnp.exp(-time_step * (anisotropy / 4.0 + total / 2.0))
    last = jnp.exp(-time_step * (anisotropy / 4.0 - total / 2.0))
    middle = factor * (cosine - half_diff * ratio)
    other = factor * (cosine + half_diff * ratio)
    cross = -factor * ratio * 0.5
    rows = [
        jnp.stack([first, zero, zero, zero]),
        jnp.stack([zero, middle, cross, zero]),
        jnp.stack([zero, cross, other, zero]),
        jnp.stack([zero, zero, zero, last]),
    ]
    return jnp.stack(rows).reshape(2, 2, 2, 2)


def apply_gate(theta, pair):
    gate = bond_gate(pair)
    rows = theta.shape[0] // 2
    width = theta.shape[1] // 2
    four = theta.reshape(rows, 2, 2, width)
    mixed = jnp.einsum("pqrs,arsc->apqc", gate, four, precision=lax.Precision.HIGHEST)
    return mixed.reshape(rows * 2, width * 2)


def truncate(left, right, start_basis, pair, rank):
    local_rows = left.shape[0]
    bond_width = right.shape[1] // 2
    left_three = left.reshape(local_rows, 2, bond_width)
    piece = lax.all_gather(right, BOND, axis=0, tiled=True)
    theta = jnp.dot(
        left_three.reshape(local_rows * 2, piece.shape[0]),
        piece,
        preferred_element_type=jnp.float32,
    )
    mixed = apply_gate(theta, pair)
    unused = (jnp.arange(start_basis.shape[1], dtype=jnp.int32) >= rank).astype(jnp.float32)
    basis = start_basis * (1.0 - unused)[None, :]
    for step in range(ITERS):
        image = jnp.dot(mixed, basis, precision=lax.Precision.HIGHEST)
        partial_cols = lax.dot_general(
            mixed, image, (((0,), (0,)), ((), ())), precision=lax.Precision.HIGHEST
        )
        cols = sum_by_parts(partial_cols, (("bond_0", "bond_1"), "bond_2"))
        gram = jnp.dot(cols.T, cols, precision=lax.Precision.HIGHEST) + jnp.diag(unused)
        chol = jnp.linalg.cholesky(gram)
        basis = lax.linalg.triangular_solve(
            chol, cols, left_side=False, lower=True, transpose_a=True
        )
    left_factor = jnp.dot(mixed, basis, precision=lax.Precision.HIGHEST)
    right_factor = jnp.sqrt(jnp.float32(mixed.shape[1])) * basis.T
    return (left_factor, right_factor)


def per_device(last_sites, first_sites, start_basis, fields, ranks):
    segment = lax.axis_index("seg")
    count = lax.axis_size("seg")
    previous = passed_along(last_sites, "seg", 1)
    owner = (segment + count - 1) % count
    left_factor, right_factor = truncate(
        previous[0], first_sites[0], start_basis, fields[owner], ranks[owner]
    )
    new_left = passed_along(left_factor[None], "seg", -1)
    new_right = right_factor[None]
    return (new_left, new_right)


def solution(mesh):
    finer = Mesh(
        mesh.devices.reshape(mesh.shape["seg"], 4, 4, 2), ("seg", "bond_0", "bond_1", "bond_2")
    )
    return jax.shard_map(
        per_device,
        mesh=finer,
        in_specs=(P("seg", BOND, None), P("seg", BOND, None), P(), P(), P()),
        out_specs=(P("seg", BOND, None), P("seg", None, None)),
        check_vma=False,
    )
```

profile of v0, /device:TPU:1, one launch (start us, length us, event | category | flops | bytes accessed | tf_op | source)
XLA Modules:
  0.0 724.9 jit_solution(5119972270818223441)
XLA Ops:
  16.1 59.0 %all-gather.3.cloned.1.call-done = bf16[1,1024,2048]{2,1,0:T(8,128)(2,1)} async-done(((bf16[1,32,2048]{2,1,0:T(8,128)(2,1)}), bf16[1,1024,2048]{2,1,0:T(8,128)(2,1)}) %all-gather.3.cloned.1.call-update) | async-done | bytes 4194320 | tf_op jit(solution)/shard_map/all_gather | solution.py:104
  100.8 34.3 %all_to_all.88 = f32[16,64,256]{2,1,0:T(8,128)} all-to-all(f32[16,64,256]{2,1,0:T(8,128)S(1)} %reduce_sum.72), channel_id=1, replica_groups=mesh['seg'=8,'bond_0'=4,'bond_1'=4,'bond_2'=2] {'bond_0','bond_1'}, dimensions={0} | all-to-all | bytes 2097152 | tf_op jit(solution)/shard_map/all_to_all | solution.py:51
  143.2 23.0 %all-to-all-done.2 = f32[16,64,256]{2,1,0:T(8,128)S(1)} async-done(((f32[16,64,256]{2,1,0:T(8,128)}), f32[16,64,256]{2,1,0:T(8,128)S(1)}, u32[]{:S(2)}, u32[]{:S(2)}) %all-to-all-start.2) | async-done | bytes 1048608 | tf_op jit(solution)/shard_map/all_to_all | solution.py:20
  178.6 11.7 %cholesky.214 = f32[128,128]{1,0:T(8,128)S(1)} custom-call(f32[128,128]{1,0:T(8,128)S(1)} %cholesky.346), custom_call_target="Cholesky" | custom-call | tf_op jit(solution)/shard_map/jit(cholesky)/cholesky | solution.py:120
  200.7 12.1 %cholesky.231 = f32[128,128]{1,0:T(8,128)S(1)} custom-call(f32[128,128]{1,0:T(8,128)S(1)} %convolution_subtract_fusion.7), custom_call_target="Cholesky" | custom-call | tf_op jit(solution)/shard_map/jit(cholesky)/cholesky | solution.py:120
  219.2 19.7 %custom-call.18 = f32[2,128,128]{1,2,0:T(8,128)S(1)} custom-call(f32[2,128,128]{2,1,0:T(8,128)S(1)} %get-tuple-element.30), custom_call_target="InvertDiagBlocksLowerTriangular" | custom-call | tf_op jit(solution)/shard_map/triangular_solve/custom-call.0 | solution.py:121
  256.9 27.8 %all_to_all.89 = f32[16,64,256]{2,1,0:T(8,128)} all-to-all(f32[16,64,256]{2,1,0:T(8,128)S(1)} %reduce_sum.74), channel_id=1, replica_groups=mesh['seg'=8,'bond_0'=4,'bond_1'=4,'bond_2'=2] {'bond_0','bond_1'}, dimensions={0} | all-to-all | bytes 2097152 | tf_op jit(solution)/shard_map/all_to_all | solution.py:51
  294.5 19.9 %all-to-all-done.6 = f32[16,64,256]{2,1,0:T(8,128)S(1)} async-done(((f32[16,64,256]{2,1,0:T(8,128)}), f32[16,64,256]{2,1,0:T(8,128)S(1)}, u32[]{:S(2)}, u32[]{:S(2)}) %all-to-all-start.6) | async-done | bytes 1048608 | tf_op jit(solution)/shard_map/all_to_all | solution.py:20
  314.6 10.1 %all_to_all.83 = f32[2,16,64,256]{3,2,1,0:T(8,128)S(1)} all-to-all(f32[2,16,64,256]{3,2,1,0:T(8,128)S(1)} %broadcast_in_dim.94), channel_id=1, replica_groups=mesh['seg'=8,'bond_0'=4,'bond_1'=4,'bond_2'=2] {'bond_2'}, dimensions={0} | all-to-all | bytes 4194304 | tf_op jit(solution)/shard_map/all_to_all | solution.py:20
  329.6 11.7 %cholesky.248 = f32[128,128]{1,0:T(8,128)S(1)} custom-call(f32[128,128]{1,0:T(8,128)S(1)} %cholesky.349), custom_call_target="Cholesky" | custom-call | tf_op jit(solution)/shard_map/jit(cholesky)/cholesky | solution.py:120
  351.7 12.1 %cholesky.265 = f32[128,128]{1,0:T(8,128)S(1)} custom-call(f32[128,128]{1,0:T(8,128)S(1)} %convolution_subtract_fusion.6), custom_call_target="Cholesky" | custom-call | tf_op jit(solution)/shard_map/jit(cholesky)/cholesky | solution.py:120
  370.2 19.7 %custom-call.20 = f32[2,128,128]{1,2,0:T(8,128)S(1)} custom-call(f32[2,128,128]{2,1,0:T(8,128)S(1)} %get-tuple-element.31), custom_call_target="InvertDiagBlocksLowerTriangular" | custom-call | tf_op jit(solution)/shard_map/triangular_solve/custom-call.0 | solution.py:121
  407.9 32.0 %all_to_all.90 = f32[16,64,256]{2,1,0:T(8,128)} all-to-all(f32[16,64,256]{2,1,0:T(8,128)S(1)} %reduce_sum.76), channel_id=1, replica_groups=mesh['seg'=8,'bond_0'=4,'bond_1'=4,'bond_2'=2] {'bond_0','bond_1'}, dimensions={0} | all-to-all | bytes 2097152 | tf_op jit(solution)/shard_map/all_to_all | solution.py:51
  449.3 18.3 %all-to-all-done.10 = f32[16,64,256]{2,1,0:T(8,128)S(1)} async-done(((f32[16,64,256]{2,1,0:T(8,128)}), f32[16,64,256]{2,1,0:T(8,128)S(1)}, u32[]{:S(2)}, u32[]{:S(2)}) %all-to-all-start.10) | async-done | bytes 1048608 | tf_op jit(solution)/shard_map/all_to_all | solution.py:20
  467.8 11.6 %all_to_all.85 = f32[2,16,64,256]{3,2,1,0:T(8,128)S(1)} all-to-all(f32[2,16,64,256]{3,2,1,0:T(8,128)S(1)} %broadcast_in_dim.96), channel_id=1, replica_groups=mesh['seg'=8,'bond_0'=4,'bond_1'=4,'bond_2'=2] {'bond_2'}, dimensions={0} | all-to-all | bytes 4194304 | tf_op jit(solution)/shard_map/all_to_all | solution.py:20
  484.4 11.7 %cholesky.282 = f32[128,128]{1,0:T(8,128)S(1)} custom-call(f32[128,128]{1,0:T(8,128)S(1)} %cholesky.352), custom_call_target="Cholesky" | custom-call | tf_op jit(solution)/shard_map/jit(cholesky)/cholesky | solution.py:120
  506.4 12.1 %cholesky.299 = f32[128,128]{1,0:T(8,128)S(1)} custom-call(f32[128,128]{1,0:T(8,128)S(1)} %convolution_subtract_fusion.5), custom_call_target="Cholesky" | custom-call | tf_op jit(solution)/shard_map/jit(cholesky)/cholesky | solution.py:120
  524.9 19.7 %custom-call.22 = f32[2,128,128]{1,2,0:T(8,128)S(1)} custom-call(f32[2,128,128]{2,1,0:T(8,128)S(1)} %get-tuple-element.32), custom_call_target="InvertDiagBlocksLowerTriangular" | custom-call | tf_op jit(solution)/shard_map/triangular_solve/custom-call.0 | solution.py:121
  562.6 32.6 %all_to_all.91 = f32[16,64,256]{2,1,0:T(8,128)S(1)} all-to-all(f32[16,64,256]{2,1,0:T(8,128)S(1)} %reduce_sum.78), channel_id=1, replica_groups=mesh['seg'=8,'bond_0'=4,'bond_1'=4,'bond_2'=2] {'bond_0','bond_1'}, dimensions={0} | all-to-all | bytes 2097152 | tf_op jit(solution)/shard_map/all_to_all | solution.py:51
  595.4 24.5 %all_to_all.92 = f32[16,64,256]{2,1,0:T(8,128)S(1)} all-to-all(f32[16,64,256]{2,1,0:T(8,128)S(1)} %broadcast_in_dim.97), channel_id=1, replica_groups=mesh['seg'=8,'bond_0'=4,'bond_1'=4,'bond_2'=2] {'bond_0','bond_1'}, dimensions={0} | all-to-all | bytes 2097152 | tf_op jit(solution)/shard_map/all_to_all | solution.py:20
  620.1 13.9 %all_to_all.87 = f32[2,16,64,256]{3,2,1,0:T(8,128)S(1)} all-to-all(f32[2,16,64,256]{3,2,1,0:T(8,128)S(1)} %broadcast_in_dim.98), channel_id=1, replica_groups=mesh['seg'=8,'bond_0'=4,'bond_1'=4,'bond_2'=2] {'bond_2'}, dimensions={0} | all-to-all | bytes 4194304 | tf_op jit(solution)/shard_map/all_to_all | solution.py:20
  639.0 11.7 %cholesky.316 = f32[128,128]{1,0:T(8,128)S(1)} custom-call(f32[128,128]{1,0:T(8,128)S(1)} %cholesky.355), custom_call_target="Cholesky" | custom-call | tf_op jit(solution)/shard_map/jit(cholesky)/cholesky | solution.py:120
  661.1 11.9 %cholesky.333 = f32[128,128]{1,0:T(8,128)S(1)} custom-call(f32[128,128]{1,0:T(8,128)S(1)} %convolution_subtract_fusion.4), custom_call_target="Cholesky" | custom-call | tf_op jit(solution)/shard_map/jit(cholesky)/cholesky | solution.py:120
  679.7 19.7 %custom-call.24 = f32[2,128,128]{1,2,0:T(8,128)S(1)} custom-call(f32[2,128,128]{2,1,0:T(8,128)S(1)} %get-tuple-element.33), custom_call_target="InvertDiagBlocksLowerTriangular" | custom-call | tf_op jit(solution)/shard_map/triangular_solve/custom-call.0 | solution.py:121
  (175 shorter events, 236.8 us)
Async XLA Ops:
  7.2 3.3 copy-start
  7.2 67.9 %all-gather.3.cloned.1.call-start = ((), (), s32[]{:S(2)}) async-start(), calls=%async_computation.16 | async-start | bytes 4325376 | tf_op jit(solution)/shard_map/all_gather | solution.py:104
  7.9 8.1 %collective-permute-start = (bf16[1,32,2048]{2,1,0:T(8,128)(2,1)}, bf16[1,32,2048]{2,1,0:T(8,128)(2,1)S(1)}, u32[]{:S(2)}, u32[]{:S(2)}) collective-permute-start(bf16[1,32,2048]{2,1,0:T(8,128)(2,1)} %param.8), channel_id=1, source_target_pairs={{0,32},{32,64},{64,96},{96,128},{128,160},{160,192},{192,224},{224... | collective-permute-start | bytes 393224 | tf_op jit(solution)/shard_map/ppermute | solution.py:64
  137.5 28.7 %all-to-all-start.2 = ((f32[16,64,256]{2,1,0:T(8,128)}), f32[16,64,256]{2,1,0:T(8,128)S(1)}, u32[]{:S(2)}, u32[]{:S(2)}) async-start(f32[16,64,256]{2,1,0:T(8,128)} %broadcast_in_dim.89), calls=%async_computation.2 | async-start | bytes 2097152 | tf_op jit(solution)/shard_map/all_to_all | solution.py:20
  173.7 1.3 copy-start.3
  287.1 27.3 %all-to-all-start.6 = ((f32[16,64,256]{2,1,0:T(8,128)}), f32[16,64,256]{2,1,0:T(8,128)S(1)}, u32[]{:S(2)}, u32[]{:S(2)}) async-start(f32[16,64,256]{2,1,0:T(8,128)} %broadcast_in_dim.93), calls=%async_computation.6 | async-start | bytes 2097152 | tf_op jit(solution)/shard_map/all_to_all | solution.py:20
  324.6 1.3 copy-start.4
  442.2 25.3 %all-to-all-start.10 = ((f32[16,64,256]{2,1,0:T(8,128)}), f32[16,64,256]{2,1,0:T(8,128)S(1)}, u32[]{:S(2)}, u32[]{:S(2)}) async-start(f32[16,64,256]{2,1,0:T(8,128)} %broadcast_in_dim.95), calls=%async_computation.10 | async-start | bytes 2097152 | tf_op jit(solution)/shard_map/all_to_all | solution.py:20
  479.4 1.3 copy-start.5
  634.0 1.3 copy-start.2
  705.2 12.6 %copy-start.1 = (f32[8,2]{0,1:T(2,128)S(1)}, f32[8,2]{0,1:T(2,128)}, u32[]{:S(2)}) copy-start(f32[8,2]{0,1:T(2,128)} %param.11) | copy-start | bytes 196
  707.2 10.0 %collective-permute-start.1 = (f32[1,64,256]{2,1,0:T(8,128)S(1)}, f32[1,64,256]{2,1,0:T(8,128)S(1)}, u32[]{:S(2)}, u32[]{:S(2)}) collective-permute-start(f32[1,64,256]{2,1,0:T(8,128)S(1)} %fusion.50), channel_id=1, source_target_pairs={{0,224},{32,0},{64,32},{96,64},{128,96},{160,128},{192,160},{224,1... | collective-permute-start | bytes 196616 | tf_op jit(solution)/shard_map/ppermute | solution.py:64
Sparse Core Ops, SparseCore 0:
  10.5 64.5 all-gather.2
where the time goes:
time: 733 us; the launch traced here: 725 us
  other arithmetic  233 us (32%)
  blocking collectives  219 us (30%)
  waiting for transfers between devices  121 us (17%)
  matrix products  55.6 us (8%)
  local copies, waits for them, and re-layouts  42.7 us (6%)
  starting transfers between devices  30.6 us (4%)
  between operations  22.7 us (3%)
    another operation x28, other arithmetic, truncate(): chol = jnp.linalg.cholesky(gram)  140 us
    all_to_all x4, blocking collectives, sum_by_axis(): lax.all_to_all(nearer, far, split_axis=0, concat_axis=0, tiled=True)  127 us
    another operation x9, other arithmetic, truncate(): lax.linalg.triangular_solve(chol, cols, left_side=False, lower=True, tran...  78.8 us
    all_to_all x5, blocking collectives, sent_to_all(): lax.all_to_all(jnp.broadcast_to(x[None], (peers, *x.shape)), axis, 0, 0,...  67.3 us
    all_to_all x3, waiting for transfers between devices, sent_to_all(): lax.all_to_all(jnp.broadcast_to(x[None], (peers, *x.shape)), axis, 0, 0,...  61.1 us
    all_gather x1, waiting for transfers between devices, truncate(): piece = lax.all_gather(right, BOND, axis=0, tiled=True)  59 us
    all_to_all x4, blocking collectives, sent_and_summed(): pieces = lax.all_to_all(split_up(x, dim, peers), axis, 0, 0, tiled=True)  25.1 us
    all_to_all x3, starting transfers between devices, sent_to_all(): lax.all_to_all(jnp.broadcast_to(x[None], (peers, *x.shape)), axis, 0, 0,...  19.6 us
  transfers between devices with their start and end apart: 6, of which 4 were waited for; matrix products, arithmetic and copies ran while one was open for 1% of the time, Pallas kernels for 0%

commit v1 on v0

--- a/solution.py
+++ b/solution.py
@@ -1,3 +1,4 @@
+import functools
 import jax
 import jax.numpy as jnp
 from jax import lax
@@ -8,6 +9,14 @@
 BOND = ("bond_0", "bond_1", "bond_2")
 time_step = 0.5
 anisotropy = 0.6
+
+
+def take_object(field, axis_no):
+    oldest = lax.all_to_all(jnp.stack([field for _ in range(lax.axis_size(BOND))]), BOND, 0, 0)
+    return jnp.concatenate(oldest, axis=axis_no)
+
+
+raise_spot_by_axis = functools.partial(take_object, axis_no=0)
 
 
 def padded_to(lines, peers):
@@ -101,7 +110,7 @@
     local_rows = left.shape[0]
     bond_width = right.shape[1] // 2
     left_three = left.reshape(local_rows, 2, bond_width)
-    piece = lax.all_gather(right, BOND, axis=0, tiled=True)
+    piece = raise_spot_by_axis(right)
     theta = jnp.dot(
         left_three.reshape(local_rows * 2, piece.shape[0]),
         piece,

time: 733 us -> 768 us (1.048)
  waiting for transfers between devices: 121 us -> 159 us
  between operations: 22.7 us -> 9.23 us
  starting transfers between devices: 30.6 us -> 40.5 us
    ppermute x2, waiting for transfers between devices: 0.01 us -> 91.1 us  [passed_along(): return lax.ppermute(x, axis, [(i, (i + by) % peers) for i in range(peers)])]
    all_gather x1 -> x0, waiting for transfers between devices: 59 us -> none  [truncate(): piece = lax.all_gather(right, BOND, axis=0, tiled=True)]
    all_to_all x0 -> x1, starting transfers between devices: none -> 12.9 us  [take_object(): lax.all_to_all(jnp.stack([field for _ in range(lax.axis_size(BOND))]), BO...]
where the time goes in v1:
time: 768 us; the launch traced here: 759 us
  other arithmetic  233 us (30%)
  blocking collectives  216 us (28%)
  waiting for transfers between devices  159 us (21%)
  matrix products  55.6 us (7%)
  local copies, waits for them, and re-layouts  45.5 us (6%)
  starting transfers between devices  40.5 us (5%)
  between operations  9.23 us (1%)
    another operation x28, other arithmetic, truncate(): chol = jnp.linalg.cholesky(gram)  140 us
    all_to_all x4, blocking collectives, sum_by_axis(): lax.all_to_all(nearer, far, split_axis=0, concat_axis=0, tiled=True)  129 us
    ppermute x2, waiting for transfers between devices, passed_along(): return lax.ppermute(x, axis, [(i, (i + by) % peers) for i in range(peers)])  91.1 us
    another operation x9, other arithmetic, truncate(): lax.linalg.triangular_solve(chol, cols, left_side=False, lower=True, tran...  78.8 us
    all_to_all x3, waiting for transfers between devices, sent_to_all(): lax.all_to_all(jnp.broadcast_to(x[None], (peers, *x.shape)), axis, 0, 0,...  68 us
    all_to_all x5, blocking collectives, sent_to_all(): lax.all_to_all(jnp.broadcast_to(x[None], (peers, *x.shape)), axis, 0, 0,...  61.6 us
    all_to_all x4, blocking collectives, sent_and_summed(): pieces = lax.all_to_all(split_up(x, dim, peers), axis, 0, 0, tiled=True)  25.6 us
    all_to_all x3, starting transfers between devices, sent_to_all(): lax.all_to_all(jnp.broadcast_to(x[None], (peers, *x.shape)), axis, 0, 0,...  16.1 us
  transfers between devices with their start and end apart: 6, of which 4 were waited for; matrix products, arithmetic and copies ran while one was open for 1% of the time, Pallas kernels for 0%

profile of v1, /device:TPU:1, one launch (start us, length us, event | category | flops | bytes accessed | tf_op | source)
XLA Modules:
  0.0 759.1 jit_solution(7470822711870439011)
XLA Ops:
  4.1 12.9 %all-to-all-start = ((bf16[32,32,2048]{2,1,0:T(8,128)(2,1)}), bf16[32,32,2048]{2,1,0:T(8,128)(2,1)}, u32[]{:S(2)}, u32[]{:S(2)}) async-start(bf16[32,32,2048]{2,1,0:T(8,128)(2,1)} %stack.46), calls=%async_computation | async-start | bytes 8388608 | tf_op jit(solution)/shard_map/all_to_all | solution.py:15
  22.6 91.1 %collective-permute-done = bf16[1,32,2048]{2,1,0:T(8,128)(2,1)S(1)} collective-permute-done((bf16[1,32,2048]{2,1,0:T(8,128)(2,1)S(1)}, bf16[1,32,2048]{2,1,0:T(8,128)(2,1)S(1)}, u32[]{:S(2)}, u32[]{:S(2)}) %collective-permute-start) | collective-permute-done | bytes 131104 | tf_op jit(solution)/shard_map/ppermute | solution.py:73
  139.9 37.4 %all_to_all.93 = f32[16,64,256]{2,1,0:T(8,128)} all-to-all(f32[16,64,256]{2,1,0:T(8,128)S(1)} %reduce_sum.72), channel_id=1, replica_groups=mesh['seg'=8,'bond_0'=4,'bond_1'=4,'bond_2'=2] {'bond_0','bond_1'}, dimensions={0} | all-to-all | bytes 2097152 | tf_op jit(solution)/shard_map/all_to_all | solution.py:60
  183.9 24.5 %all-to-all-done.3 = f32[16,64,256]{2,1,0:T(8,128)S(1)} async-done(((f32[16,64,256]{2,1,0:T(8,128)}), f32[16,64,256]{2,1,0:T(8,128)S(1)}, u32[]{:S(2)}, u32[]{:S(2)}) %all-to-all-start.3) | async-done | bytes 1048608 | tf_op jit(solution)/shard_map/all_to_all | solution.py:29
  220.8 11.7 %cholesky.214 = f32[128,128]{1,0:T(8,128)S(1)} custom-call(f32[128,128]{1,0:T(8,128)S(1)} %cholesky.346), custom_call_target="Cholesky" | custom-call | tf_op jit(solution)/shard_map/jit(cholesky)/cholesky | solution.py:129
  242.9 12.1 %cholesky.231 = f32[128,128]{1,0:T(8,128)S(1)} custom-call(f32[128,128]{1,0:T(8,128)S(1)} %convolution_subtract_fusion.7), custom_call_target="Cholesky" | custom-call | tf_op jit(solution)/shard_map/jit(cholesky)/cholesky | solution.py:129
  261.5 19.7 %custom-call.18 = f32[2,128,128]{1,2,0:T(8,128)S(1)} custom-call(f32[2,128,128]{2,1,0:T(8,128)S(1)} %get-tuple-element.30), custom_call_target="InvertDiagBlocksLowerTriangular" | custom-call | tf_op jit(solution)/shard_map/triangular_solve/custom-call.0 | solution.py:130
  299.2 31.8 %all_to_all.94 = f32[16,64,256]{2,1,0:T(8,128)} all-to-all(f32[16,64,256]{2,1,0:T(8,128)S(1)} %reduce_sum.74), channel_id=1, replica_groups=mesh['seg'=8,'bond_0'=4,'bond_1'=4,'bond_2'=2] {'bond_0','bond_1'}, dimensions={0} | all-to-all | bytes 2097152 | tf_op jit(solution)/shard_map/all_to_all | solution.py:60
  338.4 23.6 %all-to-all-done.7 = f32[16,64,256]{2,1,0:T(8,128)S(1)} async-done(((f32[16,64,256]{2,1,0:T(8,128)}), f32[16,64,256]{2,1,0:T(8,128)S(1)}, u32[]{:S(2)}, u32[]{:S(2)}) %all-to-all-start.7) | async-done | bytes 1048608 | tf_op jit(solution)/shard_map/all_to_all | solution.py:29
  374.5 11.7 %cholesky.248 = f32[128,128]{1,0:T(8,128)S(1)} custom-call(f32[128,128]{1,0:T(8,128)S(1)} %cholesky.349), custom_call_target="Cholesky" | custom-call | tf_op jit(solution)/shard_map/jit(cholesky)/cholesky | solution.py:129
  396.6 12.1 %cholesky.265 = f32[128,128]{1,0:T(8,128)S(1)} custom-call(f32[128,128]{1,0:T(8,128)S(1)} %convolution_subtract_fusion.6), custom_call_target="Cholesky" | custom-call | tf_op jit(solution)/shard_map/jit(cholesky)/cholesky | solution.py:129
  415.0 19.7 %custom-call.20 = f32[2,128,128]{1,2,0:T(8,128)S(1)} custom-call(f32[2,128,128]{2,1,0:T(8,128)S(1)} %get-tuple-element.31), custom_call_target="InvertDiagBlocksLowerTriangular" | custom-call | tf_op jit(solution)/shard_map/triangular_solve/custom-call.0 | solution.py:130
  452.7 27.7 %all_to_all.95 = f32[16,64,256]{2,1,0:T(8,128)} all-to-all(f32[16,64,256]{2,1,0:T(8,128)S(1)} %reduce_sum.76), channel_id=1, replica_groups=mesh['seg'=8,'bond_0'=4,'bond_1'=4,'bond_2'=2] {'bond_0','bond_1'}, dimensions={0} | all-to-all | bytes 2097152 | tf_op jit(solution)/shard_map/all_to_all | solution.py:60
  490.1 19.9 %all-to-all-done.11 = f32[16,64,256]{2,1,0:T(8,128)S(1)} async-done(((f32[16,64,256]{2,1,0:T(8,128)}), f32[16,64,256]{2,1,0:T(8,128)S(1)}, u32[]{:S(2)}, u32[]{:S(2)}) %all-to-all-start.11) | async-done | bytes 1048608 | tf_op jit(solution)/shard_map/all_to_all | solution.py:29
  525.3 11.7 %cholesky.282 = f32[128,128]{1,0:T(8,128)S(1)} custom-call(f32[128,128]{1,0:T(8,128)S(1)} %cholesky.352), custom_call_target="Cholesky" | custom-call | tf_op jit(solution)/shard_map/jit(cholesky)/cholesky | solution.py:129
  547.3 12.1 %cholesky.299 = f32[128,128]{1,0:T(8,128)S(1)} custom-call(f32[128,128]{1,0:T(8,128)S(1)} %convolution_subtract_fusion.5), custom_call_target="Cholesky" | custom-call | tf_op jit(solution)/shard_map/jit(cholesky)/cholesky | solution.py:129
  565.8 19.7 %custom-call.22 = f32[2,128,128]{1,2,0:T(8,128)S(1)} custom-call(f32[2,128,128]{2,1,0:T(8,128)S(1)} %get-tuple-element.32), custom_call_target="InvertDiagBlocksLowerTriangular" | custom-call | tf_op jit(solution)/shard_map/triangular_solve/custom-call.0 | solution.py:130
  603.5 31.9 %all_to_all.96 = f32[16,64,256]{2,1,0:T(8,128)S(1)} all-to-all(f32[16,64,256]{2,1,0:T(8,128)S(1)} %reduce_sum.78), channel_id=1, replica_groups=mesh['seg'=8,'bond_0'=4,'bond_1'=4,'bond_2'=2] {'bond_0','bond_1'}, dimensions={0} | all-to-all | bytes 2097152 | tf_op jit(solution)/shard_map/all_to_all | solution.py:60
  635.6 24.8 %all_to_all.97 = f32[16,64,256]{2,1,0:T(8,128)S(1)} all-to-all(f32[16,64,256]{2,1,0:T(8,128)S(1)} %broadcast_in_dim.97), channel_id=1, replica_groups=mesh['seg'=8,'bond_0'=4,'bond_1'=4,'bond_2'=2] {'bond_0','bond_1'}, dimensions={0} | all-to-all | bytes 2097152 | tf_op jit(solution)/shard_map/all_to_all | solution.py:29
  660.6 12.3 %all_to_all.92 = f32[2,16,64,256]{3,2,1,0:T(8,128)S(1)} all-to-all(f32[2,16,64,256]{3,2,1,0:T(8,128)S(1)} %broadcast_in_dim.98), channel_id=1, replica_groups=mesh['seg'=8,'bond_0'=4,'bond_1'=4,'bond_2'=2] {'bond_2'}, dimensions={0} | all-to-all | bytes 4194304 | tf_op jit(solution)/shard_map/all_to_all | solution.py:29
  677.9 11.7 %cholesky.316 = f32[128,128]{1,0:T(8,128)S(1)} custom-call(f32[128,128]{1,0:T(8,128)S(1)} %cholesky.355), custom_call_target="Cholesky" | custom-call | tf_op jit(solution)/shard_map/jit(cholesky)/cholesky | solution.py:129
  700.0 11.9 %cholesky.333 = f32[128,128]{1,0:T(8,128)S(1)} custom-call(f32[128,128]{1,0:T(8,128)S(1)} %convolution_subtract_fusion.4), custom_call_target="Cholesky" | custom-call | tf_op jit(solution)/shard_map/jit(cholesky)/cholesky | solution.py:129
  718.6 19.7 %custom-call.24 = f32[2,128,128]{1,2,0:T(8,128)S(1)} custom-call(f32[2,128,128]{2,1,0:T(8,128)S(1)} %get-tuple-element.33), custom_call_target="InvertDiagBlocksLowerTriangular" | custom-call | tf_op jit(solution)/shard_map/triangular_solve/custom-call.0 | solution.py:130
  746.1 10.6 %collective-permute-start.1 = (f32[1,64,256]{2,1,0:T(8,128)S(1)}, f32[1,64,256]{2,1,0:T(8,128)S(1)}, u32[]{:S(2)}, u32[]{:S(2)}) collective-permute-start(f32[1,64,256]{2,1,0:T(8,128)S(1)} %fusion.50), channel_id=1, source_target_pairs={{0,224},{32,0},{64,32},{96,64},{128,96},{160,128},{192,160},{224,1... | collective-permute-start | bytes 196616 | tf_op jit(solution)/shard_map/ppermute | solution.py:73
  (179 shorter events, 242.9 us)
Async XLA Ops:
  0.6 17.2 %copy-start = (f32[8,2]{0,1:T(2,128)S(1)}, f32[8,2]{0,1:T(2,128)}, u32[]{:S(2)}) copy-start(f32[8,2]{0,1:T(2,128)} %param.11) | copy-start | bytes 196
  4.0 12.9 %copy-start.6 = (bf16[1,32,2048]{2,1,0:T(8,128)(2,1)S(1)}, bf16[1,32,2048]{2,1,0:T(8,128)(2,1)}, u32[]{:S(2)}) copy-start(bf16[1,32,2048]{2,1,0:T(8,128)(2,1)} %param.8) | copy-start | bytes 393220
  4.1 17.4 %copy-start.7 = (s32[8]{0:T(128)S(1)}, s32[8]{0:T(128)}, u32[]{:S(2)}) copy-start(s32[8]{0:T(128)} %param.12) | copy-start | bytes 100
  4.1 109.7 %all-to-all-start = ((bf16[32,32,2048]{2,1,0:T(8,128)(2,1)}), bf16[32,32,2048]{2,1,0:T(8,128)(2,1)}, u32[]{:S(2)}, u32[]{:S(2)}) async-start(bf16[32,32,2048]{2,1,0:T(8,128)(2,1)} %stack.46), calls=%async_computation | async-start | bytes 8388608 | tf_op jit(solution)/shard_map/all_to_all | solution.py:15
  17.0 96.7 %collective-permute-start = (bf16[1,32,2048]{2,1,0:T(8,128)(2,1)S(1)}, bf16[1,32,2048]{2,1,0:T(8,128)(2,1)S(1)}, u32[]{:S(2)}, u32[]{:S(2)}) collective-permute-start(bf16[1,32,2048]{2,1,0:T(8,128)(2,1)S(1)} %copy-done.6), channel_id=1, source_target_pairs={{0,32},{32,64},{64,96},{96,128},{128,160},{160,192},{192,224},{224... | collective-permute-start | bytes 393224 | tf_op jit(solution)/shard_map/ppermute | solution.py:73
  179.6 28.7 %all-to-all-start.3 = ((f32[16,64,256]{2,1,0:T(8,128)}), f32[16,64,256]{2,1,0:T(8,128)S(1)}, u32[]{:S(2)}, u32[]{:S(2)}) async-start(f32[16,64,256]{2,1,0:T(8,128)} %broadcast_in_dim.89), calls=%async_computation.3 | async-start | bytes 2097152 | tf_op jit(solution)/shard_map/all_to_all | solution.py:29
  215.9 1.3 copy-start.3
  333.3 28.7 %all-to-all-start.7 = ((f32[16,64,256]{2,1,0:T(8,128)}), f32[16,64,256]{2,1,0:T(8,128)S(1)}, u32[]{:S(2)}, u32[]{:S(2)}) async-start(f32[16,64,256]{2,1,0:T(8,128)} %broadcast_in_dim.93), calls=%async_computation.7 | async-start | bytes 2097152 | tf_op jit(solution)/shard_map/all_to_all | solution.py:29
  369.5 1.3 copy-start.4
  482.8 27.2 %all-to-all-start.11 = ((f32[16,64,256]{2,1,0:T(8,128)}), f32[16,64,256]{2,1,0:T(8,128)S(1)}, u32[]{:S(2)}, u32[]{:S(2)}) async-start(f32[16,64,256]{2,1,0:T(8,128)} %broadcast_in_dim.95), calls=%async_computation.11 | async-start | bytes 2097152 | tf_op jit(solution)/shard_map/all_to_all | solution.py:29
  520.3 1.3 copy-start.5
  672.9 1.3 copy-start.2
  744.1 14.8 %copy-start.1 = (f32[8,2]{0,1:T(2,128)S(1)}, f32[8,2]{0,1:T(2,128)}, u32[]{:S(2)}) copy-start(f32[8,2]{0,1:T(2,128)} %param.11) | copy-start | bytes 196
  746.1 12.1 %collective-permute-start.1 = (f32[1,64,256]{2,1,0:T(8,128)S(1)}, f32[1,64,256]{2,1,0:T(8,128)S(1)}, u32[]{:S(2)}, u32[]{:S(2)}) collective-permute-start(f32[1,64,256]{2,1,0:T(8,128)S(1)} %fusion.50), channel_id=1, source_target_pairs={{0,224},{32,0},{64,32},{96,64},{128,96},{160,128},{192,160},{224,1... | collective-permute-start | bytes 196616 | tf_op jit(solution)/shard_map/ppermute | solution.py:73
